TPU v7x, 512 devices: a whole 4x8x8 slice. The times are simulated.
512 devices in a mesh: wide: 128 (over y, z, core), pair: 4 (over x).
Axes of the slice: x: 4, y: 8, z: 8, core: 2. Of those that a mesh axis runs over, the one named last changes fastest.
Arguments:
- blocks: bfloat16 [2048, 1024, 512], P('pair', 'wide'), may hold values from -6 to 6
- basis_a: bfloat16 [1024, 64], replicated, may hold values from -0.1875 to 0.1875
- basis_b: bfloat16 [512, 64], replicated, may hold values from -0.25 to 0.25
- sketch: bfloat16 [2048, 64], P(('pair', 'wide')), may hold values from -6 to 6
Outputs:
- transfer: float32 [4096, 64], P(('wide', 'pair'))
- coefficients: float32 [2048, 64], P(('pair', 'wide'))
All inputs are finite; a program needn't handle non-finite values.
Results may differ from a plain program's by a relative error of at most 0.0041.
Values may be sent and summed in bfloat16 or wider, within the bound.
A program may use at most 64 MiB of HBM per device.

v0:
```python
import jax
import jax.numpy as jnp
from jax import lax
from jax.sharding import PartitionSpec as P


def orthonormal(sketched, gram):
    lower = jnp.linalg.cholesky(gram)
    return lax.linalg.triangular_solve(
        lower, sketched, left_side=False, lower=True, transpose_a=True
    )


def per_device(blocks, basis_a, basis_b, sketch):
    fibres = sketch.shape[0]
    rank_a = basis_a.shape[1]
    rank_b = basis_b.shape[1]
    narrowed = jnp.einsum(
        "fac,cr->far", blocks, basis_b, preferred_element_type=jnp.float32
    ).astype(jnp.bfloat16)
    regrouped = lax.all_to_all(narrowed, "wide", split_axis=0, concat_axis=1, tiled=True)
    projected = jnp.einsum(
        "ap,far->fpr", basis_a, regrouped, preferred_element_type=jnp.float32
    ).astype(jnp.bfloat16)
    projected = projected.reshape(fibres, rank_a * rank_b)
    partial_value = jnp.einsum("fj,fk->jk", projected, sketch, preferred_element_type=jnp.float32)
    own_count = rank_a * rank_b // lax.axis_size(("wide", "pair"))
    sketch_all = lax.psum(partial_value, ("wide", "pair"))
    gram_matrix = jnp.dot(sketch_all.T, sketch_all, precision=lax.Precision.HIGHEST)
    parent_basis = orthonormal(sketch_all, gram_matrix)
    first_row = lax.axis_index(("wide", "pair")) * own_count
    own_basis = lax.dynamic_slice_in_dim(parent_basis, first_row, own_count, 0)
    transfer = own_basis * jnp.sqrt(jnp.float32(rank_a * rank_b))
    coefficients = jnp.dot(
        projected.astype(jnp.float32), parent_basis, precision=lax.Precision.HIGHEST
    )
    return (transfer, coefficients)


def solution(mesh):
    placed = (P("pair", "wide", None), P(), P(), P(("pair", "wide"), None))
    return jax.shard_map(
        per_device,
        mesh=mesh,
        in_specs=placed,
        out_specs=(P(("wide", "pair"), None), P(("pair", "wide"), None)),
        check_vma=False,
    )
```

profile of v0, /device:TPU:24, one launch (start us, length us, event | category | flops | bytes accessed | tf_op | source)
XLA Modules:
  0.0 346.8 jit_solution(4763148819996868437)
XLA Ops:
  7.2 0.0 copy-start
  7.2 0.0 all-reduce.2.cloned.1.call-start
  7.2 3.4 convolution_convert_fusion
  10.7 0.0 copy-start.1
  10.7 0.6 reshape.19
  11.3 35.6 %all_to_all.18 = bf16[128,2,1024]{2,1,0:T(2,128)(2,1)S(1)} all-to-all(bf16[128,2,1024]{2,1,0:T(2,128)(2,1)S(1)} %reshape.19), channel_id=1, replica_groups=mesh['wide'=128,'pair'=4] {'wide'}, dimensions={0} | all-to-all | bytes 1048576 | tf_op jit(solution)/shard_map/all_to_all | solution.py:21
  46.9 0.6 reshape.20
  47.5 0.0 copy-done
  47.5 0.5 fusion
  48.0 0.1 copy.19
  48.1 0.1 reshape.16
  48.2 0.0 copy-done.1
  48.2 1.4 fusion.9
  49.6 0.0 all-reduce.2.cloned.1.call-update
  49.6 271.4 %all-reduce.2.cloned.1.call-done = f32[4096,64]{0,1:T(8,128)} async-done(((f32[4096,64]{0,1:T(8,128)}), f32[4096,64]{0,1:T(8,128)}) %all-reduce.2.cloned.1.call-update) | async-done | bytes 1048592 | tf_op jit(solution)/shard_map/psum | solution.py:28
  321.0 2.5 fusion.10
  323.5 0.1 copy.20
  323.6 5.8 %cholesky.16 = f32[64,64]{1,0:T(8,128)S(1)} custom-call(f32[64,64]{1,0:T(8,128)S(1)} %fusion.8), custom_call_target="Cholesky" | custom-call | tf_op jit(solution)/shard_map/jit(cholesky)/cholesky | solution.py:8
  329.5 0.6 compare_reduce_fusion
  330.2 0.7 fusion.5
  330.8 4.9 %custom-call.6 = f32[1,64,64]{1,2,0:T(8,128)S(1)} custom-call(f32[1,64,64]{2,1,0:T(8,128)S(1)} %fusion.5), custom_call_target="InvertDiagBlocksLowerTriangular" | custom-call | tf_op jit(solution)/shard_map/triangular_solve | solution.py:9
  335.7 2.3 fusion.6
  338.0 1.2 fusion.11
  339.2 0.1 dynamic-slice_multiply_fusion
  339.3 0.7 copy.21
  (2 shorter events, 0.0 us)
Async XLA Ops:
  7.2 40.3 %copy-start = (bf16[1024,64]{0,1:T(8,128)(2,1)S(1)}, bf16[1024,64]{0,1:T(8,128)(2,1)}, u32[]{:S(2)}) copy-start(bf16[1024,64]{0,1:T(8,128)(2,1)} %param.5) | copy-start | bytes 393220
  7.2 313.8 %all-reduce.2.cloned.1.call-start = ((), (), s32[]{:S(2)}) async-start(), calls=%async_computation.1 | async-start | bytes 2097152 | tf_op jit(solution)/shard_map/psum | solution.py:28
  10.7 37.5 %copy-start.1 = (bf16[4,64]{1,0:T(4,128)(2,1)S(1)}, bf16[4,64]{1,0:T(4,128)(2,1)}, u32[]{:S(2)}) copy-start(bf16[4,64]{1,0:T(4,128)(2,1)} %param.7) | copy-start | bytes 1540
Sparse Core Ops, SparseCore 0:
  49.7 271.2 all-reduce.1
where the time goes:
time: 347 us
  waiting for transfers between devices  271 us (78%)
  blocking collectives  35.6 us (10%)
  between operations  14.1 us (4%)
  other arithmetic  12.2 us (4%)
  matrix products  11.3 us (3%)
    psum x1, waiting for transfers between devices, per_device(): sketch_all = lax.psum(partial_value, ('wide', 'pair'))  271 us
    all_to_all x1, blocking collectives, per_device(): lax.all_to_all(narrowed, 'wide', split_axis=0, concat_axis=1, tiled=True)  35.6 us
  transfers between devices with their start and end apart: 1, of which 1 were waited for; matrix products, arithmetic and copies ran while one was open for 0% of the time, Pallas kernels for 0%

commit v1 on v0

--- a/solution.py
+++ b/solution.py
@@ -25,7 +25,9 @@
     projected = projected.reshape(fibres, rank_a * rank_b)
     partial_value = jnp.einsum("fj,fk->jk", projected, sketch, preferred_element_type=jnp.float32)
     own_count = rank_a * rank_b // lax.axis_size(("wide", "pair"))
-    sketch_all = lax.psum(partial_value, ("wide", "pair"))
+    sketch_all = partial_value
+    for mesh_axis in ("pair", "wide"):
+        sketch_all = lax.psum(sketch_all, mesh_axis)
     gram_matrix = jnp.dot(sketch_all.T, sketch_all, precision=lax.Precision.HIGHEST)
     parent_basis = orthonormal(sketch_all, gram_matrix)
     first_row = lax.axis_index(("wide", "pair")) * own_count

time: 347 us -> 330 us (0.951)
  waiting for transfers between devices: 271 us -> 255 us
    psum x1 -> x2, waiting for transfers between devices: 271 us -> 255 us  [per_device(): sketch_all = lax.psum(sketch_all, mesh_axis)]
  transfers between devices with their start and end apart: 1 -> 2, of which waited for: 1 -> 2; matrix products, arithmetic and copies ran while one was open for 0% -> 0% of each run, Pallas kernels for 0% -> 0%
where the time goes in v1:
time: 330 us
  waiting for transfers between devices  255 us (77%)
  blocking collectives  35.6 us (11%)
  between operations  14.2 us (4%)
  other arithmetic  12.2 us (4%)
  matrix products  11.4 us (3%)
    psum x2, waiting for transfers between devices, per_device(): sketch_all = lax.psum(sketch_all, mesh_axis)  255 us
    all_to_all x1, blocking collectives, per_device(): lax.all_to_all(narrowed, 'wide', split_axis=0, concat_axis=1, tiled=True)  35.6 us
  transfers between devices with their start and end apart: 2, of which 2 were waited for; matrix products, arithmetic and copies ran while one was open for 0% of the time, Pallas kernels for 0%

profile of v1, /device:TPU:24, one launch (start us, length us, event | category | flops | bytes accessed | tf_op | source)
XLA Modules:
  0.0 330.1 jit_solution(7173992547782186564)
XLA Ops:
  7.2 0.0 copy-start
  7.2 0.0 all-reduce.3.cloned.1.call-start
  7.2 3.4 %convolution_convert_fusion = bf16[512,8,64]{2,1,0:T(8,128)(2,1)S(1)} fusion(bf16[512,8,512]{2,1,0:T(8,128)(2,1)} %param.4, bf16[512,64]{0,1:T(8,128)(2,1)} %param.6), kind=kOutput, calls=%fused_computation | convolution fusion | flops 268697600 | bytes 4784128 | tf_op jit(solution)/shard_map/fac,cr->far/dot_general | solution.py:18
  10.7 0.0 copy-start.1
  10.7 0.6 reshape.19
  11.3 35.6 %all_to_all.18 = bf16[128,2,1024]{2,1,0:T(2,128)(2,1)S(1)} all-to-all(bf16[128,2,1024]{2,1,0:T(2,128)(2,1)S(1)} %reshape.19), channel_id=1, replica_groups=mesh['wide'=128,'pair'=4] {'wide'}, dimensions={0} | all-to-all | bytes 1048576 | tf_op jit(solution)/shard_map/all_to_all | solution.py:21
  46.9 0.6 reshape.20
  47.5 0.0 copy-done
  47.5 0.5 fusion
  48.0 0.1 copy.19
  48.1 0.1 reshape.16
  48.2 0.0 copy-done.1
  48.2 1.4 fusion.9
  49.6 0.0 all-reduce.3.cloned.1.call-update
  49.6 0.0 all-reduce.5.cloned.1.call-start
  49.7 51.4 %all-reduce.3.cloned.1.call-done = f32[4096,64]{0,1:T(8,128)} async-done(((f32[4096,64]{0,1:T(8,128)}), f32[4096,64]{0,1:T(8,128)}) %all-reduce.3.cloned.1.call-update) | async-done | bytes 1048592 | tf_op jit(solution)/shard_map/psum | solution.py:30
  101.0 0.0 all-reduce.5.cloned.1.call-update
  101.1 203.2 %all-reduce.5.cloned.1.call-done = f32[4096,64]{0,1:T(8,128)} async-done(((f32[4096,64]{0,1:T(8,128)}), f32[4096,64]{0,1:T(8,128)}) %all-reduce.5.cloned.1.call-update) | async-done | bytes 1048592 | tf_op jit(solution)/shard_map/psum | solution.py:30
  304.2 2.6 fusion.10
  306.9 0.1 copy.20
  307.0 5.8 %cholesky.16 = f32[64,64]{1,0:T(8,128)S(1)} custom-call(f32[64,64]{1,0:T(8,128)S(1)} %fusion.8), custom_call_target="Cholesky" | custom-call | tf_op jit(solution)/shard_map/jit(cholesky)/cholesky | solution.py:8
  312.9 0.6 compare_reduce_fusion
  313.5 0.7 fusion.5
  314.2 4.9 %custom-call.6 = f32[1,64,64]{1,2,0:T(8,128)S(1)} custom-call(f32[1,64,64]{2,1,0:T(8,128)S(1)} %fusion.5), custom_call_target="InvertDiagBlocksLowerTriangular" | custom-call | tf_op jit(solution)/shard_map/triangular_solve | solution.py:9
  319.1 2.3 fusion.6
  321.3 1.2 fusion.11
  322.5 0.1 dynamic-slice_multiply_fusion
  322.6 0.7 copy.21
  (2 shorter events, 0.0 us)
Async XLA Ops:
  7.2 40.3 %copy-start = (bf16[1024,64]{0,1:T(8,128)(2,1)S(1)}, bf16[1024,64]{0,1:T(8,128)(2,1)}, u32[]{:S(2)}) copy-start(bf16[1024,64]{0,1:T(8,128)(2,1)} %param.5) | copy-start | bytes 393220
  7.2 93.8 %all-reduce.3.cloned.1.call-start = ((), (), s32[]{:S(2)}) async-start(), calls=%async_computation.1 | async-start | bytes 2097152 | tf_op jit(solution)/shard_map/psum | solution.py:30
  10.7 37.5 %copy-start.1 = (bf16[4,64]{1,0:T(4,128)(2,1)S(1)}, bf16[4,64]{1,0:T(4,128)(2,1)}, u32[]{:S(2)}) copy-start(bf16[4,64]{1,0:T(4,128)(2,1)} %param.7) | copy-start | bytes 1540
  49.6 254.6 %all-reduce.5.cloned.1.call-start = ((), (), s32[]{:S(2)}) async-start(), calls=%async_computation.2 | async-start | bytes 2097152 | tf_op jit(solution)/shard_map/psum | solution.py:30
Sparse Core Ops, SparseCore 0:
  49.7 51.2 all-reduce.2
  104.3 199.9 all-reduce.4
